TPU v7x, 32 devices: a whole 2x2x4 slice. The times are simulated.
32 devices in a mesh: grp: 2 (over y), tr: 8 (over z, x), root: 2 (over core).
Axes of the slice: x: 2, y: 2, z: 4, core: 2. Of those that a mesh axis runs over, the one named last changes fastest.
Arguments:
- residual: bfloat16 [128, 65536], P('root', ('grp', 'tr')), parts along dimension 1, may hold values from -8 to 8
- subspace: bfloat16 [512, 65536], P(None, ('grp', 'tr')), parts along dimension 1, may hold values from -1 to 1, as said below
- inverses: bfloat16 [16, 512, 512], P(('grp', 'tr')), parts along dimension 0, may hold values from -1 to 3, as said below
- owner_offset: int32 [128], P(('grp', 'tr')), parts along dimension 0, may hold values from 0 to 3, as said below
- listed: int32 [128], P(('grp', 'tr')), parts along dimension 0, may hold values from 0 to 1, as said below
Outputs:
- corrections: float32 [128, 65536], P('root', ('grp', 'tr')), parts along dimension 1
There are 2 independent parts, one for each index of `grp`. A program takes and returns all parts, laid end to end along the dimension named above; each array names one. Nothing has to cross between parts.
Inputs may be any that keep to these rules, and one draw needn't show every extreme that they name: Each entry of subspace lies within the stated range; rows are not normalized. `inverses`: each inverse is a dense real matrix. `owner_offset`: among the 8 blocks of each shard, at least one is listed and has offset 3. Each shard has at least one listed block and at least one unlisted block.
All inputs are finite; a program needn't handle non-finite values.
Results may differ from a plain program's by a relative error of at most 0.0065.
Values may be sent and summed in bfloat16 or wider, within the bound.
A program may use at most 64 MiB of HBM per device.

v0:
```python
import jax
import jax.numpy as jnp
from jax import lax
from jax.sharding import PartitionSpec as P

BLK = 512
OFFS = 4
PASSES = 2


def from_behind(block, axis, distance):
    devices = range(lax.axis_size(axis))
    route = [((i - distance) % len(devices), i) for i in devices]
    return lax.ppermute(block, axis, route)


def per_device(residual, subspace, inverses, owner_offset, listed):
    root_count, row_count = residual.shape
    block_count = row_count // BLK
    blocks = residual.reshape(root_count, block_count, BLK)
    chosen_mask = listed > 0
    inverse = inverses[0]
    target = jnp.arange(OFFS, dtype=jnp.int32)
    held_inverses = [inverse]
    for offset in range(1, OFFS):
        held_inverses.append(from_behind(inverse, "tr", -offset))
    inverse_table = jnp.stack(held_inverses)
    selector = (owner_offset[:, None] == target[None, :]).astype(jnp.bfloat16)
    picked = jnp.einsum(
        "jd,dbc->jbc", selector, inverse_table, preferred_element_type=jnp.float32
    ).astype(jnp.bfloat16)
    solved = jnp.einsum("rjb,jbc->rjc", blocks, picked, preferred_element_type=jnp.float32)
    precond = jnp.where(chosen_mask[None, :, None], solved, blocks.astype(jnp.float32)).reshape(
        root_count, row_count
    )
    current = precond
    for repeat in range(PASSES):
        rounded = current.astype(jnp.bfloat16)
        partial_correlation = lax.dot_general(
            rounded, subspace, (((1,), (1,)), ((), ())), preferred_element_type=jnp.float32
        )
        correlation = lax.psum(partial_correlation, "tr")
        coefficients = correlation.astype(jnp.bfloat16)
        current = current - jnp.dot(coefficients, subspace, preferred_element_type=jnp.float32)
    return current


def solution(mesh):
    return jax.shard_map(
        per_device,
        mesh=mesh,
        in_specs=(
            P("root", ("grp", "tr")),
            P(None, ("grp", "tr")),
            P(("grp", "tr"), None, None),
            P(("grp", "tr")),
            P(("grp", "tr")),
        ),
        out_specs=P("root", ("grp", "tr")),
        check_vma=False,
    )
```

profile of v0, /device:TPU:0, one launch (start us, length us, event | category | flops | bytes accessed | tf_op | source)
XLA Modules:
  0.0 140.2 jit_solution(10332493646921314701)
XLA Ops:
  0.0 0.0 copy-start.2
  0.0 6.0 %collective-permute-start = (bf16[512,512]{1,0:T(8,128)(2,1)}, bf16[512,512]{1,0:T(8,128)(2,1)S(1)}, u32[]{:S(2)}, u32[]{:S(2)}) collective-permute-start(bf16[512,512]{1,0:T(8,128)(2,1)} %bitcast.28), channel_id=1, source_target_pairs={{2,0},{4,2},{6,4},{8,6},{10,8},{12,10},{14,12},{0,14},{3,1},{5,3},... | collective-permute-start | bytes 1572872 | tf_op jit(solution)/shard_map/ppermute | solution.py:14
  6.0 0.4 collective-permute-start.1
  6.5 0.0 collective-permute-start.2
  6.5 0.7 broadcast_compare_fusion
  7.1 11.6 %collective-permute-done = bf16[512,512]{1,0:T(8,128)(2,1)S(1)} collective-permute-done((bf16[512,512]{1,0:T(8,128)(2,1)}, bf16[512,512]{1,0:T(8,128)(2,1)S(1)}, u32[]{:S(2)}, u32[]{:S(2)}) %collective-permute-start) | collective-permute-done | bytes 524320 | tf_op jit(solution)/shard_map/ppermute | solution.py:14
  18.7 11.2 %collective-permute-done.1 = bf16[512,512]{1,0:T(8,128)(2,1)S(1)} collective-permute-done((bf16[512,512]{1,0:T(8,128)(2,1)}, bf16[512,512]{1,0:T(8,128)(2,1)S(1)}, u32[]{:S(2)}, u32[]{:S(2)}) %collective-permute-start.1) | collective-permute-done | bytes 524320 | tf_op jit(solution)/shard_map/ppermute | solution.py:14
  29.9 10.1 %collective-permute-done.2 = bf16[512,512]{1,0:T(8,128)(2,1)S(1)} collective-permute-done((bf16[512,512]{1,0:T(8,128)(2,1)}, bf16[512,512]{1,0:T(8,128)(2,1)S(1)}, u32[]{:S(2)}, u32[]{:S(2)}) %collective-permute-start.2) | collective-permute-done | bytes 524320 | tf_op jit(solution)/shard_map/ppermute | solution.py:14
  40.0 1.3 pad_maximum_fusion
  41.3 0.0 copy-done.2
  41.3 0.0 copy-start.3
  41.3 1.5 %fusion.1 = bf16[8,512,512]{2,0,1:T(8,128)(2,1)S(1)} fusion(bf16[4,512,512]{2,1,0:T(8,128)(2,1)S(1)} %pad_maximum_fusion, s32[8]{0:T(128)S(1)} %copy-done.2), kind=kOutput, calls=%fused_computation.5 | convolution fusion | flops 16777248 | bytes 6291488 | tf_op jit(solution)/shard_map/jd,dbc->jbc/dot_general | solution.py:29
  42.9 0.0 copy-done.3
  42.9 0.0 copy-start
  42.9 2.5 %fusion.5 = f32[8,8,8,512]{3,2,1,0:T(8,128)S(1)} fusion(bf16[8,512,512]{2,0,1:T(8,128)(2,1)S(1)} %fusion.1, bf16[8,8,8,512]{3,2,1,0:T(8,128)(2,1)S(1)} %bitcast.34, pred[8]{0:T(512)(128)(4,1)S(1)} %broadcast_compare_fusion), kind=kOutput, calls=%fused_computation.9 | convolution fusion | flops 268959744 | bytes 5767176 | tf_op jit(solution)/shard_map/rjb,jbc->rjc/dot_general | solution.py:32
  45.4 0.1 copy.12
  45.4 0.0 copy-done
  45.5 1.4 %fusion.10 = f32[64,512]{1,0:T(8,128)S(1)} fusion(bf16[512,4096]{1,0:T(8,128)(2,1)S(1)} %copy-done, f32[64,4096]{1,0:T(8,128)S(1)} %bitcast.26), kind=kOutput, calls=%fused_computation.14 | convolution fusion | flops 268697600 | bytes 5373952 | tf_op jit(solution)/shard_map/dot_general | solution.py:39
  46.9 50.4 %all-reduce.2 = bf16[64,512]{1,0:T(8,128)(2,1)S(1)} all-reduce(f32[64,512]{1,0:T(8,128)S(1)} %fusion.10), channel_id=1, replica_groups=mesh['grp'=2,'tr'=8,'root'=2] {'tr'}, use_global_device_ids=true, to_apply=%region_0.1 | all-reduce | flops 32768 | bytes 196608 | tf_op jit(solution)/shard_map/psum | solution.py:42
  97.2 0.0 copy-start.1
  97.2 3.2 %convolution_subtract_fusion.1 = f32[64,4096]{1,0:T(8,128)S(1)} fusion(f32[64,4096]{1,0:T(8,128)S(1)} %bitcast.27, bf16[512,4096]{1,0:T(8,128)(2,1)} %param.6, bf16[64,512]{1,0:T(8,128)(2,1)S(1)} %all-reduce.2), kind=kOutput, calls=%fused_computation.2 | convolution fusion | flops 268697600 | bytes 6356992 | tf_op jit(solution)/shard_map/dot_general | solution.py:44
  100.4 0.3 copy-done.1
  100.7 1.4 fusion.8
  102.1 34.1 %all-reduce.3 = bf16[64,512]{1,0:T(8,128)(2,1)S(1)} all-reduce(f32[64,512]{1,0:T(8,128)S(1)} %fusion.8), channel_id=1, replica_groups=mesh['grp'=2,'tr'=8,'root'=2] {'tr'}, use_global_device_ids=true, to_apply=%region_1.2 | all-reduce | flops 32768 | bytes 196608 | tf_op jit(solution)/shard_map/psum | solution.py:42
  136.2 4.0 %convolution_subtract_fusion = f32[64,4096]{1,0:T(8,128)} fusion(f32[64,4096]{1,0:T(8,128)S(1)} %convolution_subtract_fusion.1, bf16[512,4096]{1,0:T(8,128)(2,1)} %param.6, bf16[64,512]{1,0:T(8,128)(2,1)S(1)} %all-reduce.3), kind=kOutput, calls=%fused_computation.1 | convolution fusion | flops 268697600 | bytes 6356992 | tf_op jit(solution)/shard_map/dot_general | solution.py:44
Async XLA Ops:
  0.0 41.3 %copy-start.2 = (s32[8]{0:T(128)S(1)}, s32[8]{0:T(128)}, u32[]{:S(2)}) copy-start(s32[8]{0:T(128)} %param.8) | copy-start | bytes 100
  0.0 18.7 %collective-permute-start = (bf16[512,512]{1,0:T(8,128)(2,1)}, bf16[512,512]{1,0:T(8,128)(2,1)S(1)}, u32[]{:S(2)}, u32[]{:S(2)}) collective-permute-start(bf16[512,512]{1,0:T(8,128)(2,1)} %bitcast.28), channel_id=1, source_target_pairs={{2,0},{4,2},{6,4},{8,6},{10,8},{12,10},{14,12},{0,14},{3,1},{5,3},... | collective-permute-start | bytes 1572872 | tf_op jit(solution)/shard_map/ppermute | solution.py:14
  6.0 23.9 %collective-permute-start.1 = (bf16[512,512]{1,0:T(8,128)(2,1)}, bf16[512,512]{1,0:T(8,128)(2,1)S(1)}, u32[]{:S(2)}, u32[]{:S(2)}) collective-permute-start(bf16[512,512]{1,0:T(8,128)(2,1)} %bitcast.29), channel_id=1, source_target_pairs={{4,0},{6,2},{8,4},{10,6},{12,8},{14,10},{0,12},{2,14},{5,1},{7,3},... | collective-permute-start | bytes 1572872 | tf_op jit(solution)/shard_map/ppermute | solution.py:14
  6.5 33.6 %collective-permute-start.2 = (bf16[512,512]{1,0:T(8,128)(2,1)}, bf16[512,512]{1,0:T(8,128)(2,1)S(1)}, u32[]{:S(2)}, u32[]{:S(2)}) collective-permute-start(bf16[512,512]{1,0:T(8,128)(2,1)} %bitcast.30), channel_id=1, source_target_pairs={{6,0},{8,2},{10,4},{12,6},{14,8},{0,10},{2,12},{4,14},{7,1},{9,3},... | collective-permute-start | bytes 1572872 | tf_op jit(solution)/shard_map/ppermute | solution.py:14
  41.3 1.5 %copy-start.3 = (bf16[64,4096]{1,0:T(8,128)(2,1)S(1)}, bf16[64,4096]{1,0:T(8,128)(2,1)}, u32[]{:S(2)}) copy-start(bf16[64,4096]{1,0:T(8,128)(2,1)} %param.5) | copy-start | bytes 1572868
  42.9 2.6 %copy-start = (bf16[512,4096]{1,0:T(8,128)(2,1)S(1)}, bf16[512,4096]{1,0:T(8,128)(2,1)}, u32[]{:S(2)}) copy-start(bf16[512,4096]{1,0:T(8,128)(2,1)} %param.6) | copy-start | bytes 12582916
  97.2 3.5 %copy-start.1 = (bf16[512,4096]{1,0:T(8,128)(2,1)S(1)}, bf16[512,4096]{1,0:T(8,128)(2,1)}, u32[]{:S(2)}) copy-start(bf16[512,4096]{1,0:T(8,128)(2,1)} %param.6) | copy-start | bytes 12582916
where the time goes:
time: 140 us
  blocking collectives  84.5 us (60%)
  waiting for transfers between devices  32.9 us (24%)
  matrix products  14 us (10%)
  starting transfers between devices  6.46 us (5%)
  other arithmetic  1.96 us (1%)
    psum x2, blocking collectives, per_device(): correlation = lax.psum(partial_correlation, 'tr')  84.5 us
    ppermute x3, waiting for transfers between devices, from_behind(): return lax.ppermute(block, axis, route)  32.9 us
    dot_general x2, matrix products, per_device(): jnp.dot(coefficients, subspace, preferred_element_type=jnp.float32)  7.19 us
    ppermute x3, starting transfers between devices, from_behind(): return lax.ppermute(block, axis, route)  6.46 us
    dot_general x2, matrix products, per_device(): lax.dot_general(rounded, subspace, (((1,), (1,)), ((), ())), preferred_el...  2.8 us
  transfers between devices with their start and end apart: 3, of which 3 were waited for; matrix products, arithmetic and copies ran while one was open for 0% of the time, Pallas kernels for 0%

commit v1 on v0

--- a/solution.py
+++ b/solution.py
@@ -39,7 +39,11 @@
         partial_correlation = lax.dot_general(
             rounded, subspace, (((1,), (1,)), ((), ())), preferred_element_type=jnp.float32
         )
-        correlation = lax.psum(partial_correlation, "tr")
+        correlation = partial_correlation
+        for hop in (1, 2, 4):
+            correlation = correlation + lax.ppermute(
+                correlation, "tr", [(dev, dev ^ hop) for dev in range(8)]
+            )
         coefficients = correlation.astype(jnp.bfloat16)
         current = current - jnp.dot(coefficients, subspace, preferred_element_type=jnp.float32)
     return current

time: 140 us -> 98.3 us (0.70)
  blocking collectives: 84.5 us -> 0 us
  waiting for transfers between devices: 32.9 us -> 57.7 us
  starting transfers between devices: 6.46 us -> 28.8 us
  matrix products: 14 us -> 9.44 us
    psum x2 -> x0, blocking collectives: 84.5 us -> none  [per_device(): correlation = lax.psum(partial_correlation, 'tr')]
    ppermute x0 -> x6, waiting for transfers between devices: none -> 24.8 us  [per_device(): lax.ppermute(correlation, 'tr', [(dev, dev ^ hop) for dev in range(8)])]
    ppermute x0 -> x6, starting transfers between devices: none -> 22.3 us  [per_device(): lax.ppermute(correlation, 'tr', [(dev, dev ^ hop) for dev in range(8)])]
    dot_general x2, matrix products: 7.19 us -> 2.66 us  [per_device(): jnp.dot(coefficients, subspace, preferred_element_type=jnp.float32)]
  transfers between devices with their start and end apart: 3 -> 9, of which waited for: 3 -> 9; matrix products, arithmetic and copies ran while one was open for 0% -> 1% of each run, Pallas kernels for 0% -> 0%
where the time goes in v1:
time: 98.3 us; the launch traced here: 98.1 us
  waiting for transfers between devices  57.7 us (59%)
  starting transfers between devices  28.8 us (29%)
  matrix products  9.44 us (10%)
  other arithmetic  2.04 us (2%)
    ppermute x3, waiting for transfers between devices, from_behind(): return lax.ppermute(block, axis, route)  32.9 us
    ppermute x6, waiting for transfers between devices, per_device(): lax.ppermute(correlation, 'tr', [(dev, dev ^ hop) for dev in range(8)])  24.8 us
    ppermute x6, starting transfers between devices, per_device(): lax.ppermute(correlation, 'tr', [(dev, dev ^ hop) for dev in range(8)])  22.3 us
    ppermute x3, starting transfers between devices, from_behind(): return lax.ppermute(block, axis, route)  6.46 us
    dot_general x2, matrix products, per_device(): lax.dot_general(rounded, subspace, (((1,), (1,)), ((), ())), preferred_el...  2.79 us
    dot_general x2, matrix products, per_device(): jnp.dot(coefficients, subspace, preferred_element_type=jnp.float32)  2.66 us
    dot_general x1, matrix products, per_device(): jnp.einsum('rjb,jbc->rjc', blocks, picked, preferred_element_type=jnp.flo...  2.46 us
  transfers between devices with their start and end apart: 9, of which 9 were waited for; matrix products, arithmetic and copies ran while one was open for 1% of the time, Pallas kernels for 0%

profile of v1, /device:TPU:0, one launch (start us, length us, event | category | flops | bytes accessed | tf_op | source)
XLA Modules:
  0.0 98.1 jit_solution(16321838392906028172)
XLA Ops:
  0.0 6.0 %collective-permute-start = (bf16[512,512]{1,0:T(8,128)(2,1)}, bf16[512,512]{1,0:T(8,128)(2,1)S(1)}, u32[]{:S(2)}, u32[]{:S(2)}) collective-permute-start(bf16[512,512]{1,0:T(8,128)(2,1)} %bitcast.26), channel_id=1, source_target_pairs={{2,0},{4,2},{6,4},{8,6},{10,8},{12,10},{14,12},{0,14},{3,1},{5,3},... | collective-permute-start | bytes 1572872 | tf_op jit(solution)/shard_map/ppermute | solution.py:14
  6.0 0.4 collective-permute-start.1
  6.5 0.0 collective-permute-start.2
  6.5 0.7 broadcast_compare_fusion
  7.1 11.6 %collective-permute-done = bf16[512,512]{1,0:T(8,128)(2,1)S(1)} collective-permute-done((bf16[512,512]{1,0:T(8,128)(2,1)}, bf16[512,512]{1,0:T(8,128)(2,1)S(1)}, u32[]{:S(2)}, u32[]{:S(2)}) %collective-permute-start) | collective-permute-done | bytes 524320 | tf_op jit(solution)/shard_map/ppermute | solution.py:14
  18.7 11.2 %collective-permute-done.1 = bf16[512,512]{1,0:T(8,128)(2,1)S(1)} collective-permute-done((bf16[512,512]{1,0:T(8,128)(2,1)}, bf16[512,512]{1,0:T(8,128)(2,1)S(1)}, u32[]{:S(2)}, u32[]{:S(2)}) %collective-permute-start.1) | collective-permute-done | bytes 524320 | tf_op jit(solution)/shard_map/ppermute | solution.py:14
  29.9 10.1 %collective-permute-done.2 = bf16[512,512]{1,0:T(8,128)(2,1)S(1)} collective-permute-done((bf16[512,512]{1,0:T(8,128)(2,1)}, bf16[512,512]{1,0:T(8,128)(2,1)S(1)}, u32[]{:S(2)}, u32[]{:S(2)}) %collective-permute-start.2) | collective-permute-done | bytes 524320 | tf_op jit(solution)/shard_map/ppermute | solution.py:14
  40.0 1.3 %pad_maximum_fusion = bf16[4,512,512]{2,1,0:T(8,128)(2,1)S(1)} fusion(bf16[1,512,512]{2,1,0:T(8,128)(2,1)S(1)} %bitcast.31, bf16[1,512,512]{2,1,0:T(8,128)(2,1)S(1)} %bitcast.30, bf16[1,512,512]{2,1,0:T(8,128)(2,1)S(1)} %bitcast.29, bf16[1,512,512]{2,1,0:T(8,128)(2,1)} %param.7), kind=kLoop, calls=%fused_computation.4 | loop fusion | flops 3145728 | bytes 4194304 | tf_op jit(solution)/shard_map/stack | solution.py:27
  41.3 0.0 copy-done.1
  41.3 0.0 copy-start.2
  41.3 1.5 %fusion.1 = bf16[8,512,512]{2,0,1:T(8,128)(2,1)S(1)} fusion(bf16[4,512,512]{2,1,0:T(8,128)(2,1)S(1)} %pad_maximum_fusion, s32[8]{0:T(128)S(1)} %copy-done.1), kind=kOutput, calls=%fused_computation.5 | convolution fusion | flops 16777248 | bytes 6291488 | tf_op jit(solution)/shard_map/jd,dbc->jbc/dot_general | solution.py:29
  42.9 0.0 copy-done.2
  42.9 0.0 copy-start
  42.9 2.5 %fusion.5 = f32[8,8,8,512]{3,2,1,0:T(8,128)S(1)} fusion(bf16[8,512,512]{2,0,1:T(8,128)(2,1)S(1)} %fusion.1, bf16[8,8,8,512]{3,2,1,0:T(8,128)(2,1)S(1)} %bitcast.32, pred[8]{0:T(512)(128)(4,1)S(1)} %broadcast_compare_fusion), kind=kOutput, calls=%fused_computation.9 | convolution fusion | flops 268959744 | bytes 5767176 | tf_op jit(solution)/shard_map/rjb,jbc->rjc/dot_general | solution.py:32
  45.4 0.1 copy.12
  45.5 0.0 copy-done
  45.5 1.4 %fusion.10 = f32[64,512]{1,0:T(8,128)S(1)} fusion(bf16[512,4096]{1,0:T(8,128)(2,1)S(1)} %copy-done, f32[64,4096]{1,0:T(8,128)S(1)} %bitcast.24), kind=kOutput, calls=%fused_computation.14 | convolution fusion | flops 268697600 | bytes 5373952 | tf_op jit(solution)/shard_map/dot_general | solution.py:39
  46.9 12.5 %collective-permute-start.3 = (f32[64,512]{1,0:T(8,128)S(1)}, f32[64,512]{1,0:T(8,128)S(1)}, u32[]{:S(2)}, u32[]{:S(2)}) collective-permute-start(f32[64,512]{1,0:T(8,128)S(1)} %fusion.10), channel_id=1, source_target_pairs={{0,2},{2,0},{4,6},{6,4},{8,10},{10,8},{12,14},{14,12},{1,3},{3,1},... | collective-permute-start | bytes 393224 | tf_op jit(solution)/shard_map/ppermute | solution.py:44
  59.4 2.9 %collective-permute-done.3 = f32[64,512]{1,0:T(8,128)S(1)} collective-permute-done((f32[64,512]{1,0:T(8,128)S(1)}, f32[64,512]{1,0:T(8,128)S(1)}, u32[]{:S(2)}, u32[]{:S(2)}) %collective-permute-start.3) | collective-permute-done | bytes 131104 | tf_op jit(solution)/shard_map/ppermute | solution.py:44
  62.3 2.7 %collective-permute-start.4 = (f32[64,512]{1,0:T(8,128)S(1)}, f32[64,512]{1,0:T(8,128)S(1)}, u32[]{:S(2)}, u32[]{:S(2)}) collective-permute-start(f32[64,512]{1,0:T(8,128)S(1)} %add.18), channel_id=1, source_target_pairs={{0,4},{2,6},{4,0},{6,2},{8,12},{10,14},{12,8},{14,10},{1,5},{3,7},... | collective-permute-start | bytes 393224 | tf_op jit(solution)/shard_map/ppermute | solution.py:44
  65.1 2.9 %collective-permute-done.4 = f32[64,512]{1,0:T(8,128)S(1)} collective-permute-done((f32[64,512]{1,0:T(8,128)S(1)}, f32[64,512]{1,0:T(8,128)S(1)}, u32[]{:S(2)}, u32[]{:S(2)}) %collective-permute-start.4) | collective-permute-done | bytes 131104 | tf_op jit(solution)/shard_map/ppermute | solution.py:44
  68.1 3.2 %collective-permute-start.5 = (f32[64,512]{1,0:T(8,128)S(1)}, f32[64,512]{1,0:T(8,128)S(1)}, u32[]{:S(2)}, u32[]{:S(2)}) collective-permute-start(f32[64,512]{1,0:T(8,128)S(1)} %add.19), channel_id=1, source_target_pairs={{0,8},{2,10},{4,12},{6,14},{8,0},{10,2},{12,4},{14,6},{1,9},{3,11}... | collective-permute-start | bytes 393224 | tf_op jit(solution)/shard_map/ppermute | solution.py:44
  71.3 5.3 %collective-permute-done.5 = f32[64,512]{1,0:T(8,128)S(1)} collective-permute-done((f32[64,512]{1,0:T(8,128)S(1)}, f32[64,512]{1,0:T(8,128)S(1)}, u32[]{:S(2)}, u32[]{:S(2)}) %collective-permute-start.5) | collective-permute-done | bytes 131104 | tf_op jit(solution)/shard_map/ppermute | solution.py:44
  76.6 0.8 convolution_subtract_fusion.1
  77.5 1.4 %fusion.8 = f32[64,512]{1,0:T(8,128)S(1)} fusion(bf16[512,4096]{1,0:T(8,128)(2,1)S(1)} %copy-done, f32[64,4096]{1,0:T(8,128)S(1)} %convolution_subtract_fusion.1), kind=kOutput, calls=%fused_computation.12 | convolution fusion | flops 268697600 | bytes 5373952 | tf_op jit(solution)/shard_map/dot_general | solution.py:39
  78.9 1.1 %collective-permute-start.6 = (f32[64,512]{1,0:T(8,128)S(1)}, f32[64,512]{1,0:T(8,128)S(1)}, u32[]{:S(2)}, u32[]{:S(2)}) collective-permute-start(f32[64,512]{1,0:T(8,128)S(1)} %fusion.8), channel_id=1, source_target_pairs={{0,2},{2,0},{4,6},{6,4},{8,10},{10,8},{12,14},{14,12},{1,3},{3,1},... | collective-permute-start | bytes 393224 | tf_op jit(solution)/shard_map/ppermute | solution.py:44
  79.9 4.0 %collective-permute-done.6 = f32[64,512]{1,0:T(8,128)S(1)} collective-permute-done((f32[64,512]{1,0:T(8,128)S(1)}, f32[64,512]{1,0:T(8,128)S(1)}, u32[]{:S(2)}, u32[]{:S(2)}) %collective-permute-start.6) | collective-permute-done | bytes 131104 | tf_op jit(solution)/shard_map/ppermute | solution.py:44
  83.9 0.6 collective-permute-start.7
  84.5 4.4 %collective-permute-done.7 = f32[64,512]{1,0:T(8,128)S(1)} collective-permute-done((f32[64,512]{1,0:T(8,128)S(1)}, f32[64,512]{1,0:T(8,128)S(1)}, u32[]{:S(2)}, u32[]{:S(2)}) %collective-permute-start.7) | collective-permute-done | bytes 131104 | tf_op jit(solution)/shard_map/ppermute | solution.py:44
  89.0 2.2 %collective-permute-start.8 = (f32[64,512]{1,0:T(8,128)S(1)}, f32[64,512]{1,0:T(8,128)S(1)}, u32[]{:S(2)}, u32[]{:S(2)}) collective-permute-start(f32[64,512]{1,0:T(8,128)S(1)} %add.22), channel_id=1, source_target_pairs={{0,8},{2,10},{4,12},{6,14},{8,0},{10,2},{12,4},{14,6},{1,9},{3,11}... | collective-permute-start | bytes 393224 | tf_op jit(solution)/shard_map/ppermute | solution.py:44
  91.1 5.2 %collective-permute-done.8 = f32[64,512]{1,0:T(8,128)S(1)} collective-permute-done((f32[64,512]{1,0:T(8,128)S(1)}, f32[64,512]{1,0:T(8,128)S(1)}, u32[]{:S(2)}, u32[]{:S(2)}) %collective-permute-start.8) | collective-permute-done | bytes 131104 | tf_op jit(solution)/shard_map/ppermute | solution.py:44
  96.3 1.8 %convolution_subtract_fusion = f32[64,4096]{1,0:T(8,128)} fusion(f32[64,4096]{1,0:T(8,128)S(1)} %convolution_subtract_fusion.1, bf16[512,4096]{1,0:T(8,128)(2,1)S(1)} %copy-done, f32[64,512]{1,0:T(8,128)S(1)} %add.22, f32[64,512]{1,0:T(8,128)S(1)} %collective-permute-done.8), kind=kOutput, calls=%fused_computation.1 | convolution fusion | flops 268763136 | bytes 6553600 | tf_op jit(solution)/shard_map/dot_general | solution.py:48
  (5 shorter events, 0.1 us)
Async XLA Ops:
  0.0 41.3 %copy-start.1 = (s32[8]{0:T(128)S(1)}, s32[8]{0:T(128)}, u32[]{:S(2)}) copy-start(s32[8]{0:T(128)} %param.8) | copy-start | bytes 100
  0.0 18.7 %collective-permute-start = (bf16[512,512]{1,0:T(8,128)(2,1)}, bf16[512,512]{1,0:T(8,128)(2,1)S(1)}, u32[]{:S(2)}, u32[]{:S(2)}) collective-permute-start(bf16[512,512]{1,0:T(8,128)(2,1)} %bitcast.26), channel_id=1, source_target_pairs={{2,0},{4,2},{6,4},{8,6},{10,8},{12,10},{14,12},{0,14},{3,1},{5,3},... | collective-permute-start | bytes 1572872 | tf_op jit(solution)/shard_map/ppermute | solution.py:14
  6.0 23.9 %collective-permute-start.1 = (bf16[512,512]{1,0:T(8,128)(2,1)}, bf16[512,512]{1,0:T(8,128)(2,1)S(1)}, u32[]{:S(2)}, u32[]{:S(2)}) collective-permute-start(bf16[512,512]{1,0:T(8,128)(2,1)} %bitcast.27), channel_id=1, source_target_pairs={{4,0},{6,2},{8,4},{10,6},{12,8},{14,10},{0,12},{2,14},{5,1},{7,3},... | collective-permute-start | bytes 1572872 | tf_op jit(solution)/shard_map/ppermute | solution.py:14
  6.5 33.6 %collective-permute-start.2 = (bf16[512,512]{1,0:T(8,128)(2,1)}, bf16[512,512]{1,0:T(8,128)(2,1)S(1)}, u32[]{:S(2)}, u32[]{:S(2)}) collective-permute-start(bf16[512,512]{1,0:T(8,128)(2,1)} %bitcast.28), channel_id=1, source_target_pairs={{6,0},{8,2},{10,4},{12,6},{14,8},{0,10},{2,12},{4,14},{7,1},{9,3},... | collective-permute-start | bytes 1572872 | tf_op jit(solution)/shard_map/ppermute | solution.py:14
  41.3 1.5 %copy-start.2 = (bf16[64,4096]{1,0:T(8,128)(2,1)S(1)}, bf16[64,4096]{1,0:T(8,128)(2,1)}, u32[]{:S(2)}) copy-start(bf16[64,4096]{1,0:T(8,128)(2,1)} %param.5) | copy-start | bytes 1572868
  42.9 2.6 %copy-start = (bf16[512,4096]{1,0:T(8,128)(2,1)S(1)}, bf16[512,4096]{1,0:T(8,128)(2,1)}, u32[]{:S(2)}) copy-start(bf16[512,4096]{1,0:T(8,128)(2,1)} %param.6) | copy-start | bytes 12582916
  46.9 15.5 %collective-permute-start.3 = (f32[64,512]{1,0:T(8,128)S(1)}, f32[64,512]{1,0:T(8,128)S(1)}, u32[]{:S(2)}, u32[]{:S(2)}) collective-permute-start(f32[64,512]{1,0:T(8,128)S(1)} %fusion.10), channel_id=1, source_target_pairs={{0,2},{2,0},{4,6},{6,4},{8,10},{10,8},{12,14},{14,12},{1,3},{3,1},... | collective-permute-start | bytes 393224 | tf_op jit(solution)/shard_map/ppermute | solution.py:44
  62.3 5.7 %collective-permute-start.4 = (f32[64,512]{1,0:T(8,128)S(1)}, f32[64,512]{1,0:T(8,128)S(1)}, u32[]{:S(2)}, u32[]{:S(2)}) collective-permute-start(f32[64,512]{1,0:T(8,128)S(1)} %add.18), channel_id=1, source_target_pairs={{0,4},{2,6},{4,0},{6,2},{8,12},{10,14},{12,8},{14,10},{1,5},{3,7},... | collective-permute-start | bytes 393224 | tf_op jit(solution)/shard_map/ppermute | solution.py:44
  68.1 8.6 %collective-permute-start.5 = (f32[64,512]{1,0:T(8,128)S(1)}, f32[64,512]{1,0:T(8,128)S(1)}, u32[]{:S(2)}, u32[]{:S(2)}) collective-permute-start(f32[64,512]{1,0:T(8,128)S(1)} %add.19), channel_id=1, source_target_pairs={{0,8},{2,10},{4,12},{6,14},{8,0},{10,2},{12,4},{14,6},{1,9},{3,11}... | collective-permute-start | bytes 393224 | tf_op jit(solution)/shard_map/ppermute | solution.py:44
  78.9 5.0 %collective-permute-start.6 = (f32[64,512]{1,0:T(8,128)S(1)}, f32[64,512]{1,0:T(8,128)S(1)}, u32[]{:S(2)}, u32[]{:S(2)}) collective-permute-start(f32[64,512]{1,0:T(8,128)S(1)} %fusion.8), channel_id=1, source_target_pairs={{0,2},{2,0},{4,6},{6,4},{8,10},{10,8},{12,14},{14,12},{1,3},{3,1},... | collective-permute-start | bytes 393224 | tf_op jit(solution)/shard_map/ppermute | solution.py:44
  83.9 5.0 %collective-permute-start.7 = (f32[64,512]{1,0:T(8,128)S(1)}, f32[64,512]{1,0:T(8,128)S(1)}, u32[]{:S(2)}, u32[]{:S(2)}) collective-permute-start(f32[64,512]{1,0:T(8,128)S(1)} %add.21), channel_id=1, source_target_pairs={{0,4},{2,6},{4,0},{6,2},{8,12},{10,14},{12,8},{14,10},{1,5},{3,7},... | collective-permute-start | bytes 393224 | tf_op jit(solution)/shard_map/ppermute | solution.py:44
  89.0 7.3 %collective-permute-start.8 = (f32[64,512]{1,0:T(8,128)S(1)}, f32[64,512]{1,0:T(8,128)S(1)}, u32[]{:S(2)}, u32[]{:S(2)}) collective-permute-start(f32[64,512]{1,0:T(8,128)S(1)} %add.22), channel_id=1, source_target_pairs={{0,8},{2,10},{4,12},{6,14},{8,0},{10,2},{12,4},{14,6},{1,9},{3,11}... | collective-permute-start | bytes 393224 | tf_op jit(solution)/shard_map/ppermute | solution.py:44
